TPU v7x, 256 devices: a whole 4x4x8 slice. The times are simulated.
256 devices in a mesh: particle: 16 (over y, z_hi), coeffici: 8 (over x, core), half: 2 (over z_lo).
Axes of the slice: x: 4, y: 4, z: 8 (z_hi: 4, z_lo: 2; z = z_hi * 2 + z_lo), core: 2. Of those that a mesh axis runs over, the one named last changes fastest.
Arguments:
- residuals: float32 [2, 16384, 16384], P('half', 'particle', 'coeffici'), may hold values from -6 to 6
- loadings: float32 [2, 16384, 256], P('half', 'coeffici'), may hold values from -0.046875 to 0.046875
Outputs:
- new_loadings: float32 [2, 16384, 256], P('half', ('coeffici', 'particle'))
- rayleigh: float32 [2, 256, 256], P('half')
All inputs are finite; a program needn't handle non-finite values.
Results may differ from a plain program's by a relative error of at most 0.00024.
Values sent between devices are 32-bit elements; how exact they have to be, the bound alone decides.
No kernel may reach another device: no remote copies, remote signals or barrier semaphores. Data moves between devices by JAX's collectives and lax.ppermute only.
A program may use at most 64 MiB of HBM per device.

v0:
```python
import math
import jax
import jax.numpy as jnp
from jax import lax
from jax.sharding import PartitionSpec as P


def from_partner(value, axis, distance):
    mask = 2**distance
    pairs = [(source, source ^ mask) for source in range(lax.axis_size(axis))]
    return lax.ppermute(value, axis, pairs)


def contract_rows(left, right):
    return lax.dot_general(
        left,
        right,
        (((0,), (0,)), ((), ())),
        precision=lax.Precision.HIGHEST,
        preferred_element_type=jnp.float32,
    )


def local(residuals, loadings):
    samples = residuals[0]
    loading = loadings[0]
    factor = 1.0 / math.sqrt(samples.shape[0] * lax.axis_size("particle"))
    partial_value = jnp.dot(
        samples, loading, precision=lax.Precision.HIGHEST, preferred_element_type=jnp.float32
    )
    scores = lax.psum(partial_value, "coeffici")
    share_rows = samples.shape[1] // lax.axis_size("particle")
    first_row = lax.axis_index("particle") * share_rows
    local_cov = contract_rows(samples, scores)
    covariance = lax.psum(local_cov, "particle") * factor
    partner = from_partner(covariance, "half", 0)
    shrunk = covariance * jax.nn.sigmoid(covariance * partner)
    correlation = contract_rows(loading, shrunk)
    rayleigh = lax.psum(correlation, "coeffici") * factor
    weighted = lax.dynamic_slice_in_dim(shrunk, first_row, share_rows, 0)
    return (weighted[None], rayleigh[None])


def solution(mesh):
    in_specs = (P("half", "particle", "coeffici"), P("half", "coeffici", None))
    out_specs = (P("half", ("coeffici", "particle"), None), P("half", None, None))
    return jax.shard_map(local, mesh=mesh, in_specs=in_specs, out_specs=out_specs, check_vma=False)
```

profile of v0, /device:TPU:8, one launch (start us, length us, event | category | flops | bytes accessed | tf_op | source)
XLA Modules:
  0.0 395.9 jit_solution(12921856936748713425)
XLA Ops:
  7.2 0.0 copy-start
  7.2 0.0 all-reduce.4.cloned.1.call-start
  7.2 1.5 copy-done
  8.8 9.9 %fusion.2 = f32[1024,256]{1,0:T(8,128)} fusion(f32[1,1024,2048]{2,1,0:T(8,128)} %param.2, f32[1,2048,256]{2,1,0:T(8,128)S(1)} %copy-done), kind=kOutput, calls=%fused_computation.2 | convolution fusion | flops 6442450944 | bytes 11534336 | tf_op jit(solution)/shard_map/dot_general | solution.py:28
  18.6 0.0 all-reduce.4.cloned.1.call-update
  18.7 0.0 all-reduce.6.cloned.1.call-start
  18.7 70.6 %all-reduce.4.cloned.1.call-done = f32[1024,256]{1,0:T(8,128)} async-done(((f32[1024,256]{1,0:T(8,128)}), f32[1024,256]{1,0:T(8,128)}) %all-reduce.4.cloned.1.call-update) | async-done | bytes 1048592 | tf_op jit(solution)/shard_map/psum | solution.py:31
  89.3 10.7 %fusion.4 = f32[2048,256]{0,1:T(8,128)} fusion(f32[1024,256]{1,0:T(8,128)} %all-reduce.4.cloned.1.call-done, f32[1,1024,2048]{2,1,0:T(8,128)} %param.2), kind=kOutput, calls=%fused_computation.4 | convolution fusion | flops 6442450944 | bytes 11534336 | tf_op jit(solution)/shard_map/dot_general | solution.py:15
  100.1 0.0 all-reduce.6.cloned.1.call-update
  100.1 0.0 all-reduce.8.cloned.1.call-start
  100.1 175.1 %all-reduce.6.cloned.1.call-done = f32[2048,256]{0,1:T(8,128)} async-done(((f32[2048,256]{0,1:T(8,128)}), f32[2048,256]{0,1:T(8,128)}) %all-reduce.6.cloned.1.call-update) | async-done | bytes 2097168 | tf_op jit(solution)/shard_map/psum | solution.py:35
  275.3 1.9 broadcast_multiply_fusion
  277.2 2.2 collective-permute-start
  279.3 38.0 %collective-permute-done = f32[2048,256]{0,1:T(8,128)S(1)} collective-permute-done((f32[2048,256]{0,1:T(8,128)S(1)}, f32[2048,256]{0,1:T(8,128)S(1)}, u32[]{:S(2)}, u32[]{:S(2)}) %collective-permute-start) | collective-permute-done | bytes 2097184 | tf_op jit(solution)/shard_map/ppermute | solution.py:11
  317.3 0.0 copy-done.2
  317.3 0.9 divide_multiply_fusion
  318.3 1.3 copy-done.1
  319.6 2.6 fusion.10
  322.2 0.0 all-reduce.8.cloned.1.call-update
  322.2 0.9 constant_dynamic-slice_fusion
  323.2 0.8 copy.5
  323.9 63.6 %all-reduce.8.cloned.1.call-done = f32[256,256]{0,1:T(8,128)} async-done(((f32[256,256]{0,1:T(8,128)}), f32[256,256]{0,1:T(8,128)}) %all-reduce.8.cloned.1.call-update) | async-done | bytes 262160 | tf_op jit(solution)/shard_map/psum | solution.py:39
  387.5 1.0 multiply_bitcast_fusion
  388.5 0.8 copy.6
  (2 shorter events, 0.0 us)
Async XLA Ops:
  7.2 1.6 copy-start
  7.2 82.2 %all-reduce.4.cloned.1.call-start = ((), (), s32[]{:S(2)}) async-start(), calls=%async_computation | async-start | bytes 2097152 | tf_op jit(solution)/shard_map/psum | solution.py:31
  18.7 256.6 %all-reduce.6.cloned.1.call-start = ((), (), s32[]{:S(2)}) async-start(), calls=%async_computation.1 | async-start | bytes 4194304 | tf_op jit(solution)/shard_map/psum | solution.py:35
  100.1 287.4 %all-reduce.8.cloned.1.call-start = ((), (), s32[]{:S(2)}) async-start(), calls=%async_computation.2 | async-start | bytes 524288 | tf_op jit(solution)/shard_map/psum | solution.py:39
  275.3 42.1 %copy-start.2 = (f32[2048,256]{0,1:T(8,128)S(1)}, f32[2048,256]{0,1:T(8,128)}, u32[]{:S(2)}) copy-start(f32[2048,256]{0,1:T(8,128)} %all-reduce.6.cloned.1.call-done) | copy-start | bytes 6291460
  277.2 40.2 %collective-permute-start = (f32[2048,256]{0,1:T(8,128)S(1)}, f32[2048,256]{0,1:T(8,128)S(1)}, u32[]{:S(2)}, u32[]{:S(2)}) collective-permute-start(f32[2048,256]{0,1:T(8,128)S(1)} %broadcast_multiply_fusion), channel_id=1, source_target_pairs={{0,1},{1,0},{2,3},{3,2},{4,5},{5,4},{6,7},{7,6},{8,9},{9,8},{10,11... | collective-permute-start | bytes 6291464 | tf_op jit(solution)/shard_map/ppermute | solution.py:11
  318.3 1.3 copy-start.1
Sparse Core Ops, SparseCore 0:
  18.8 70.5 all-reduce.3
  100.2 175.0 all-reduce.5
  322.3 65.1 all-reduce.7
where the time goes:
time: 396 us
  waiting for transfers between devices  347 us (88%)
  matrix products  23.2 us (6%)
  between operations  13.8 us (3%)
  local copies, waits for them, and re-layouts  5.38 us (1%)
    psum x1, waiting for transfers between devices, local(): covariance = lax.psum(local_cov, 'particle') * factor  175 us
    psum x1, waiting for transfers between devices, local(): scores = lax.psum(partial_value, 'coeffici')  70.6 us
    psum x1, waiting for transfers between devices, local(): rayleigh = lax.psum(correlation, 'coeffici') * factor  63.6 us
    ppermute x1, waiting for transfers between devices, from_partner(): return lax.ppermute(value, axis, pairs)  38 us
    dot_general x2, matrix products, contract_rows(): lax.dot_general(left, right, (((0,), (0,)), ((), ())), precision=lax.Prec...  13.3 us
    dot_general x1, matrix products, local(): jnp.dot(samples, loading, precision=lax.Precision.HIGHEST, preferred_elem...  9.87 us
  transfers between devices with their start and end apart: 4, of which 4 were waited for; matrix products, arithmetic and copies ran while one was open for 0% of the time, Pallas kernels for 0%

commit v1 on v0

--- a/solution.py
+++ b/solution.py
@@ -28,7 +28,9 @@
     partial_value = jnp.dot(
         samples, loading, precision=lax.Precision.HIGHEST, preferred_element_type=jnp.float32
     )
-    scores = lax.psum(partial_value, "coeffici")
+    scores = partial_value
+    for hop in (1, 2, 4):
+        scores = scores + lax.ppermute(scores, "coeffici", [(dev, dev ^ hop) for dev in range(8)])
     share_rows = samples.shape[1] // lax.axis_size("particle")
     first_row = lax.axis_index("particle") * share_rows
     local_cov = contract_rows(samples, scores)

time: 396 us -> 382 us (0.965)
  waiting for transfers between devices: 347 us -> 329 us
  starting transfers between devices: 2.28 us -> 7.18 us
    psum x1 -> x0, waiting for transfers between devices: 70.6 us -> none  [local(): scores = lax.psum(partial_value, 'coeffici')]
    ppermute x0 -> x3, waiting for transfers between devices: none -> 49.2 us  [local(): lax.ppermute(scores, 'coeffici', [(dev, dev ^ hop) for dev in range(8)])]
    ppermute x0 -> x3, starting transfers between devices: none -> 4.95 us  [local(): lax.ppermute(scores, 'coeffici', [(dev, dev ^ hop) for dev in range(8)])]
  transfers between devices with their start and end apart: 4 -> 6, of which waited for: 4 -> 6; matrix products, arithmetic and copies ran while one was open for 0% -> 0% of each run, Pallas kernels for 0% -> 0%
where the time goes in v1:
time: 382 us; the launch traced here: 381 us
  waiting for transfers between devices  329 us (86%)
  matrix products  21.1 us (6%)
  between operations  14.1 us (4%)
  starting transfers between devices  7.18 us (2%)
  local copies, waits for them, and re-layouts  5.4 us (1%)
  other arithmetic  4.05 us (1%)
    psum x1, waiting for transfers between devices, local(): covariance = lax.psum(local_cov, 'particle') * factor  179 us
    psum x1, waiting for transfers between devices, local(): rayleigh = lax.psum(correlation, 'coeffici') * factor  63.6 us
    ppermute x3, waiting for transfers between devices, local(): lax.ppermute(scores, 'coeffici', [(dev, dev ^ hop) for dev in range(8)])  49.2 us
    ppermute x1, waiting for transfers between devices, from_partner(): return lax.ppermute(value, axis, pairs)  38 us
    dot_general x2, matrix products, contract_rows(): lax.dot_general(left, right, (((0,), (0,)), ((), ())), precision=lax.Prec...  11.2 us
    dot_general x1, matrix products, local(): jnp.dot(samples, loading, precision=lax.Precision.HIGHEST, preferred_elem...  9.96 us
  transfers between devices with their start and end apart: 6, of which 6 were waited for; matrix products, arithmetic and copies ran while one was open for 0% of the time, Pallas kernels for 0%

profile of v1, /device:TPU:8, one launch (start us, length us, event | category | flops | bytes accessed | tf_op | source)
XLA Modules:
  0.0 381.4 jit_solution(5462337412020420330)
XLA Ops:
  7.2 1.5 copy-done
  8.8 10.0 %fusion.2 = f32[1024,256]{1,0:T(8,128)S(1)} fusion(f32[1,1024,2048]{2,1,0:T(8,128)} %param.2, f32[1,2048,256]{2,1,0:T(8,128)S(1)} %copy-done), kind=kOutput, calls=%fused_computation.2 | convolution fusion | flops 6442450944 | bytes 11534336 | tf_op jit(solution)/shard_map/dot_general | solution.py:28
  18.7 0.1 collective-permute-start
  18.8 2.6 collective-permute-done
  21.5 0.1 add.19
  21.6 1.6 collective-permute-start.1
  23.2 23.7 %collective-permute-done.1 = f32[1024,256]{1,0:T(8,128)S(1)} collective-permute-done((f32[1024,256]{1,0:T(8,128)S(1)}, f32[1024,256]{1,0:T(8,128)S(1)}, u32[]{:S(2)}, u32[]{:S(2)}) %collective-permute-start.1) | collective-permute-done | bytes 1048608 | tf_op jit(solution)/shard_map/ppermute | solution.py:33
  46.9 0.1 add.20
  47.0 3.3 collective-permute-start.2
  50.3 22.8 %collective-permute-done.2 = f32[1024,256]{1,0:T(8,128)S(1)} collective-permute-done((f32[1024,256]{1,0:T(8,128)S(1)}, f32[1024,256]{1,0:T(8,128)S(1)}, u32[]{:S(2)}, u32[]{:S(2)}) %collective-permute-start.2) | collective-permute-done | bytes 1048608 | tf_op jit(solution)/shard_map/ppermute | solution.py:33
  73.2 8.6 %fusion.4 = f32[2048,256]{0,1:T(8,128)} fusion(f32[1,1024,2048]{2,1,0:T(8,128)S(1)} %copy-done.1, f32[1024,256]{1,0:T(8,128)S(1)} %add.20, f32[1024,256]{1,0:T(8,128)S(1)} %collective-permute-done.2), kind=kOutput, calls=%fused_computation.4 | convolution fusion | flops 6442713088 | bytes 12582912 | tf_op jit(solution)/shard_map/dot_general | solution.py:15
  81.7 0.0 all-reduce.5.cloned.1.call-start
  81.8 178.7 %all-reduce.3.cloned.1.call-done = f32[2048,256]{0,1:T(8,128)} async-done(((f32[2048,256]{0,1:T(8,128)}), f32[2048,256]{0,1:T(8,128)}) %all-reduce.3.cloned.1.call-update) | async-done | bytes 2097168 | tf_op jit(solution)/shard_map/psum | solution.py:37
  260.5 1.9 broadcast_multiply_fusion
  262.4 2.2 collective-permute-start.3
  264.5 38.0 %collective-permute-done.3 = f32[2048,256]{0,1:T(8,128)S(1)} collective-permute-done((f32[2048,256]{0,1:T(8,128)S(1)}, f32[2048,256]{0,1:T(8,128)S(1)}, u32[]{:S(2)}, u32[]{:S(2)}) %collective-permute-start.3) | collective-permute-done | bytes 2097184 | tf_op jit(solution)/shard_map/ppermute | solution.py:11
  302.5 0.9 divide_multiply_fusion
  303.5 1.3 copy-done.2
  304.8 2.6 fusion.10
  307.4 0.9 constant_dynamic-slice_fusion
  308.4 0.8 copy.5
  309.1 63.6 %all-reduce.5.cloned.1.call-done = f32[256,256]{0,1:T(8,128)} async-done(((f32[256,256]{0,1:T(8,128)}), f32[256,256]{0,1:T(8,128)}) %all-reduce.5.cloned.1.call-update) | async-done | bytes 262160 | tf_op jit(solution)/shard_map/psum | solution.py:41
  372.7 1.0 multiply_bitcast_fusion
  373.7 0.8 copy.6
  (9 shorter events, 0.1 us)
Async XLA Ops:
  7.2 1.6 copy-start
  7.2 253.3 %all-reduce.3.cloned.1.call-start = ((), (), s32[]{:S(2)}) async-start(), calls=%async_computation | async-start | bytes 4194304 | tf_op jit(solution)/shard_map/psum | solution.py:37
  8.8 64.4 %copy-start.1 = (f32[1,1024,2048]{2,1,0:T(8,128)S(1)}, f32[1,1024,2048]{2,1,0:T(8,128)}, u32[]{:S(2)}) copy-start(f32[1,1024,2048]{2,1,0:T(8,128)} %param.2) | copy-start | bytes 25165828
  18.7 2.7 collective-permute-start
  21.6 25.3 %collective-permute-start.1 = (f32[1024,256]{1,0:T(8,128)S(1)}, f32[1024,256]{1,0:T(8,128)S(1)}, u32[]{:S(2)}, u32[]{:S(2)}) collective-permute-start(f32[1024,256]{1,0:T(8,128)S(1)} %add.19), channel_id=1, source_target_pairs={{0,4},{2,6},{4,0},{6,2},{8,12},{10,14},{12,8},{14,10},{1,5},{3,7},... | collective-permute-start | bytes 3145736 | tf_op jit(solution)/shard_map/ppermute | solution.py:33
  47.0 26.1 %collective-permute-start.2 = (f32[1024,256]{1,0:T(8,128)S(1)}, f32[1024,256]{1,0:T(8,128)S(1)}, u32[]{:S(2)}, u32[]{:S(2)}) collective-permute-start(f32[1024,256]{1,0:T(8,128)S(1)} %add.20), channel_id=1, source_target_pairs={{0,8},{2,10},{4,12},{6,14},{8,0},{10,2},{12,4},{14,6},{1,9},{3,11}... | collective-permute-start | bytes 3145736 | tf_op jit(solution)/shard_map/ppermute | solution.py:33
  81.7 291.0 %all-reduce.5.cloned.1.call-start = ((), (), s32[]{:S(2)}) async-start(), calls=%async_computation.1 | async-start | bytes 524288 | tf_op jit(solution)/shard_map/psum | solution.py:41
  260.5 42.1 %copy-start.3 = (f32[2048,256]{0,1:T(8,128)S(1)}, f32[2048,256]{0,1:T(8,128)}, u32[]{:S(2)}) copy-start(f32[2048,256]{0,1:T(8,128)} %all-reduce.3.cloned.1.call-done) | copy-start | bytes 6291460
  262.4 40.2 %collective-permute-start.3 = (f32[2048,256]{0,1:T(8,128)S(1)}, f32[2048,256]{0,1:T(8,128)S(1)}, u32[]{:S(2)}, u32[]{:S(2)}) collective-permute-start(f32[2048,256]{0,1:T(8,128)S(1)} %broadcast_multiply_fusion), channel_id=1, source_target_pairs={{0,1},{1,0},{2,3},{3,2},{4,5},{5,4},{6,7},{7,6},{8,9},{9,8},{10,11... | collective-permute-start | bytes 6291464 | tf_op jit(solution)/shard_map/ppermute | solution.py:11
  303.4 1.3 copy-start.2
Sparse Core Ops, SparseCore 0:
  81.9 178.5 all-reduce.2
  307.6 65.1 all-reduce.4
